TPU v7x, 32 devices: a whole 2x2x4 slice. The times are simulated.
32 devices in a mesh: seq: 16 (over z, y, x), head: 2 (over core).
Axes of the slice: x: 2, y: 2, z: 4, core: 2. Of those that a mesh axis runs over, the one named last changes fastest.
Arguments:
- x_in: bfloat16 [2816, 1024], P('seq'), may hold values from -7 to 7
- seg_ids: int32 [2816], replicated, may hold values from 0 to 6, never falling along the last dimension, each value on 1 to 2112 neighbouring positions
- decay_exp: int32 [24], P('head'), may hold values from 3 to 16
- cotangent: bfloat16 [2816, 1024], P('seq'), may hold values from -6 to 6
- w_zx: bfloat16 [1024, 2, 1536], P('seq', None, 'head'), may hold values from -0.1875 to 0.1875
- w_bc: bfloat16 [1024, 256], P('seq'), may hold values from -0.1875 to 0.1875
- w_dt: bfloat16 [1024, 24], P('seq', 'head'), may hold values from -0.1875 to 0.1875
- w_mout: bfloat16 [1536, 1024], P('head', 'seq'), may hold values from -0.15625 to 0.15625
- w_q: bfloat16 [1024, 512], P('seq', 'head'), may hold values from -0.1875 to 0.1875
- w_kv: bfloat16 [1024, 2, 128], P('seq', None, 'head'), may hold values from -0.1875 to 0.1875
- w_ao: bfloat16 [512, 1024], P('head', 'seq'), may hold values from -3.5 to 3.5
- w_gu: bfloat16 [1024, 2, 2048], P('seq', None, 'head'), may hold values from -0.1875 to 0.1875
- w_down: bfloat16 [2048, 1024], P('head', 'seq'), may hold values from -0.125 to 0.125
- norm1_gain: float32 [1024], replicated, may hold values from 0.25 to 1.75
- norm2_gain: float32 [1024], replicated, may hold values from 0.25 to 1.75
- mnorm_gain: float32 [1536], P('head'), may hold values from 0.25 to 1.75
- conv_x: float32 [4, 1536], P(None, 'head'), may hold values from -3 to 3
- conv_bc: float32 [4, 256], replicated, may hold values from -3 to 3
- dt_bias: float32 [24], P('head'), may hold values from -2 to 1
- skip_d: float32 [24], P('head'), may hold values from 0.5 to 1.5
Outputs:
- output: bfloat16 [2816, 1024], P('seq')
- x_grad: float32 [2816, 1024], P('seq')
- w_zx_grad: float32 [1024, 2, 1536], P('seq', None, 'head')
- w_bc_grad: float32 [1024, 256], P('seq')
- w_dt_grad: float32 [1024, 24], P('seq', 'head')
- w_mout_grad: float32 [1536, 1024], P('head', 'seq')
- w_q_grad: float32 [1024, 512], P('seq', 'head')
- w_kv_grad: float32 [1024, 2, 128], P('seq', None, 'head')
- w_ao_grad: float32 [512, 1024], P('head', 'seq')
- w_gu_grad: float32 [1024, 2, 2048], P('seq', None, 'head')
- w_down_grad: float32 [2048, 1024], P('head', 'seq')
- norm1_gain_grad: float32 [1024], replicated
- norm2_gain_grad: float32 [1024], replicated
- mnorm_gain_grad: float32 [1536], P('head')
- conv_x_grad: float32 [4, 1536], P(None, 'head')
- conv_bc_grad: float32 [4, 256], replicated
- dt_bias_grad: float32 [24], P('head')
- skip_d_grad: float32 [24], P('head')
Inputs may be any that keep to these rules, and one draw needn't show every extreme that they name: `seg_ids`: sequence ids never fall along the tokens; every id is used, each sequence holds at most 2112 consecutive tokens, and some sequence holds exactly 2112.
All inputs are finite; a program needn't handle non-finite values.
Results may differ from a plain program's by a relative error of at most 0.01225.
The roundings to bfloat16 on the way count: a program that leaves them out, or rounds other values in their place, can miss the bound.
Values may be sent and summed in bfloat16 or wider, within the bound.
A program may use at most 256 MiB of HBM per device.

v0:
```python
import jax
import jax.numpy as jnp
from jax import lax
from jax.sharding import PartitionSpec as P

MI = 1536
MP = 64
NS = 128
AD = 64
TOK_DEV = 176


epsilon = 1e-05
key_multiplier = 0.390625
attention_multiplier = 0.9375
mamba_multiplier = 0.5
gate_multiplier = 0.75
down_multiplier = 0.5
rope_base = 100000000000.0
far_below = -1e30
highest = lax.Precision.HIGHEST
group_blocks = 4


def from_behind(block, axis, distance):
    devices = range(lax.axis_size(axis))
    route = [(i - distance, i) for i in devices if i - distance in devices]
    return lax.ppermute(block, axis, route)


def entering(part, axis, combine, identity, reverse):
    count = lax.axis_size(axis)
    place = lax.axis_index(axis)
    ahead = count - 1 - place if reverse else place
    gathered = jax.tree.map(lambda a: lax.all_gather(a, axis), part)
    state = jax.tree.map(lambda a, e: jnp.zeros_like(a) + jnp.asarray(e, a.dtype), part, identity)

    def one(hop, state):
        source = count - 1 - hop if reverse else hop
        return combine(
            state, jax.tree.map(lambda a: lax.dynamic_index_in_dim(a, source, 0, False), gathered)
        )

    return lax.fori_loop(0, ahead, one, state)


def silu_grad(values):
    sigmoid_value = jax.nn.sigmoid(values)
    return sigmoid_value * (1.0 + values * (1.0 - sigmoid_value))


def rotate(values, positions, direction):
    half_dim = values.shape[-1] // 2
    frequency = jnp.power(
        jnp.float32(rope_base), -jnp.arange(half_dim, dtype=jnp.float32) / half_dim
    )
    angles = positions.astype(jnp.float32)[:, None] * frequency[None, :]
    cosine = jnp.cos(angles)[:, None, :]
    sine_part = direction * jnp.sin(angles)[:, None, :]
    first_half = values[..., :half_dim]
    second_half = values[..., half_dim:]
    return jnp.concatenate(
        [
            first_half * cosine - second_half * sine_part,
            second_half * cosine + first_half * sine_part,
        ],
        axis=-1,
    )


def conv_masks(conv_seg, tap_count):
    row_count = conv_seg.shape[0] - tap_count + 1
    own_seg = conv_seg[tap_count - 1 :]
    return [
        conv_seg[tap_index : tap_index + row_count] == own_seg for tap_index in range(tap_count)
    ]


def conv_apply(extended, keep_list, weight):
    row_count = keep_list[0].shape[0]
    result = jnp.zeros((row_count, extended.shape[1]), jnp.float32)
    for tap_index in range(weight.shape[0]):
        result = result + weight[tap_index][None, :] * jnp.where(
            keep_list[tap_index][:, None], extended[tap_index : tap_index + row_count], 0.0
        )
    return result


def conv_grads(extended, keep_list, weight, grad_pre):
    row_count = grad_pre.shape[0]
    grad_ext = jnp.zeros(extended.shape, jnp.float32)
    weight_parts = []
    for tap_index in range(weight.shape[0]):
        masked = jnp.where(keep_list[tap_index][:, None], grad_pre, 0.0)
        grad_ext = grad_ext.at[tap_index : tap_index + row_count].add(
            weight[tap_index][None, :] * masked
        )
        weight_parts.append(jnp.sum(masked * extended[tap_index : tap_index + row_count], axis=0))
    return (grad_ext, jnp.stack(weight_parts))


def lower_ones(row_count):
    row_ids = jnp.arange(row_count, dtype=jnp.int32)
    return (row_ids[:, None] >= row_ids[None, :]).astype(jnp.float32)


def ssd_out(
    channels, b_matrix, c_matrix, log_decay, step_size, state_in, skip_gain, pair_keep, first_keep
):
    row_count, head_count = log_decay.shape
    cumulative = jnp.dot(lower_ones(row_count), log_decay, precision=highest)
    cum_heads = cumulative.T
    difference = cum_heads[:, :, None] - cum_heads[:, None, :]
    decay_matrix = jnp.where(
        pair_keep[None], jnp.exp(jnp.where(pair_keep[None], difference, 0.0)), 0.0
    )
    inner_product = jnp.dot(c_matrix, b_matrix.T, precision=highest)
    mixing = decay_matrix * inner_product[None]
    inputs = channels.reshape(row_count, head_count, -1)
    scaled = inputs * step_size[:, :, None]
    result = jnp.einsum("hts,shp->thp", mixing, scaled, precision=highest)
    carried = jnp.einsum("tn,hpn->thp", c_matrix, state_in, precision=highest)
    result = (
        result
        + (jnp.exp(cumulative) * first_keep[:, None])[:, :, None] * carried
        + skip_gain[None, :, None] * inputs
    )
    return result.reshape(row_count, -1)


def ssd_end(channels, b_matrix, log_decay, step_size, state_in, first_keep, last_keep):
    row_count, head_count = log_decay.shape
    cumulative = jnp.dot(lower_ones(row_count), log_decay, precision=highest)
    whole_sum = cumulative[-1]
    tail_decay = jnp.exp(whole_sum[None, :] - cumulative) * last_keep[:, None]
    scaled = channels.reshape(row_count, head_count, -1) * (step_size * tail_decay)[:, :, None]
    end_state = jnp.einsum("thp,tn->hpn", scaled, b_matrix, precision=highest)
    carry_factor = jnp.exp(whole_sum) * first_keep[-1]
    return (end_state + carry_factor[:, None, None] * state_in, carry_factor)


def combine_affine(earlier, later):
    return (earlier[0] * later[0], later[0][:, None, None] * earlier[1] + later[1])


def step_plan(reach_blocks):
    plan_list = []
    held_blocks = 1
    while held_blocks < reach_blocks:
        extra_blocks = min(held_blocks, reach_blocks - held_blocks)
        plan_list.append((held_blocks, extra_blocks))
        held_blocks = held_blocks + extra_blocks
    return plan_list


def double_window(kv_send, reach_blocks, tok_rows):
    held = kv_send
    for held_blocks, extra_blocks in step_plan(reach_blocks):
        arrived = from_behind(held[(held_blocks - extra_blocks) * tok_rows :], "seq", held_blocks)
        held = jnp.concatenate([arrived, held], 0)
    return held


def double_back(window_grads, reach_blocks, tok_rows):
    running = window_grads
    for held_blocks, extra_blocks in reversed(step_plan(reach_blocks)):
        arrived_part = running[: extra_blocks * tok_rows]
        kept_part = running[extra_blocks * tok_rows :]
        returned = from_behind(arrived_part.astype(jnp.bfloat16), "seq", -held_blocks).astype(
            arrived_part.dtype
        )
        running = kept_part.at[(held_blocks - extra_blocks) * tok_rows :].add(returned)
    return running


def attend(query_rows, window_kv, keep_mask, group_rows, group_total):
    q_heads = query_rows.shape[1]
    tok_rows = query_rows.shape[0]
    top_init = jnp.full((q_heads, tok_rows, 1), far_below, jnp.float32)
    total_init = jnp.zeros((q_heads, tok_rows, 1), jnp.float32)

    def group_scores(group_index):
        start = group_index * group_rows
        group_kv = lax.dynamic_slice_in_dim(window_kv, start, group_rows)
        group_mask = lax.dynamic_slice_in_dim(keep_mask, start, group_rows, 1)
        scores = jnp.einsum(
            "tgd,kd->gtk", query_rows, group_kv[:, :AD], preferred_element_type=jnp.float32
        ) * AD ** (-0.5)
        return (scores, group_kv, group_mask)

    def first_pass(group_index, carried):

        def first_live(state):
            row_top, total = state
            scores, _, group_mask = group_scores(group_index)
            masked = jnp.where(group_mask[None], scores, far_below)
            new_top = jnp.maximum(row_top, jnp.max(masked, axis=-1, keepdims=True))
            new_total = total * jnp.exp(row_top - new_top) + jnp.sum(
                jnp.exp(masked - new_top), axis=-1, keepdims=True
            )
            return (new_top, new_total)

        mask_here = lax.dynamic_slice_in_dim(keep_mask, group_index * group_rows, group_rows, 1)
        return lax.cond(jnp.any(mask_here), first_live, lambda state: state, carried)

    row_top, total = lax.fori_loop(0, group_total, first_pass, (top_init, total_init))
    log_sum = row_top + jnp.log(total)

    def second_pass(group_index, acc):

        def second_live(acc_in):
            scores, group_kv, group_mask = group_scores(group_index)
            probabilities = jnp.exp(
                jnp.where(group_mask[None], scores - log_sum, far_below)
            ).astype(jnp.bfloat16)
            return acc_in + jnp.einsum(
                "gtk,kd->tgd", probabilities, group_kv[:, AD:], preferred_element_type=jnp.float32
            )

        mask_here = lax.dynamic_slice_in_dim(keep_mask, group_index * group_rows, group_rows, 1)
        return lax.cond(jnp.any(mask_here), second_live, lambda acc_in: acc_in, acc)

    result = lax.fori_loop(
        0, group_total, second_pass, jnp.zeros((tok_rows, q_heads, AD), jnp.float32)
    )
    return (result.astype(jnp.bfloat16), log_sum)


def attend_back(query_rows, window_kv, keep_mask, log_sum, out_rows, grad_rows):
    key_rows = window_kv[:, :AD]
    value_rows = window_kv[:, AD:]
    scores = jnp.einsum(
        "tgd,kd->gtk", query_rows, key_rows, preferred_element_type=jnp.float32
    ) * AD ** (-0.5)
    probabilities = jnp.exp(jnp.where(keep_mask[None], scores - log_sum, far_below))
    row_delta = jnp.sum(grad_rows.astype(jnp.float32) * out_rows.astype(jnp.float32), axis=-1).T
    grad_probs = jnp.einsum(
        "tgd,kd->gtk", grad_rows, value_rows, preferred_element_type=jnp.float32
    )
    grad_scores = (probabilities * (grad_probs - row_delta[:, :, None])).astype(jnp.bfloat16)
    probs_rounded = probabilities.astype(jnp.bfloat16)
    grad_query = jnp.einsum(
        "gtk,kd->tgd", grad_scores, key_rows, preferred_element_type=jnp.float32
    ) * AD ** (-0.5)
    grad_keys = jnp.einsum(
        "gtk,tgd->kd", grad_scores, query_rows, preferred_element_type=jnp.float32
    ) * AD ** (-0.5)
    grad_values = jnp.einsum(
        "gtk,tgd->kd", probs_rounded, grad_rows, preferred_element_type=jnp.float32
    )
    return (grad_query, jnp.concatenate([grad_keys, grad_values], axis=-1))


def product_t(left, right):
    return jnp.einsum("tc,td->cd", left, right, preferred_element_type=jnp.float32)


def local(
    x_in,
    seg_ids,
    decay_exp,
    cotangent,
    w_zx,
    w_bc,
    w_dt,
    w_mout,
    w_q,
    w_kv,
    w_ao,
    w_gu,
    w_down,
    norm1_gain,
    norm2_gain,
    mnorm_gain,
    conv_x,
    conv_bc,
    dt_bias,
    skip_d,
):
    tok_rows = x_in.shape[0]
    seq_count = lax.axis_size("seq")
    reach_blocks = tok_rows * seq_count * 3 // 4 // tok_rows + 1
    window_blocks = (reach_blocks + group_blocks - 1) // group_blocks * group_blocks
    lead_blocks = window_blocks - reach_blocks
    group_total = window_blocks // group_blocks
    group_rows = group_blocks * tok_rows
    tap_count = conv_x.shape[0]
    pad_rows = window_blocks * tok_rows
    seq_index = lax.axis_index("seq")
    start_row = seq_index * tok_rows
    token_ids = jnp.arange(tok_rows, dtype=jnp.int32)
    positions = start_row + token_ids
    seg_front = jnp.concatenate([jnp.full((pad_rows,), -1, jnp.int32), seg_ids])
    own_seg = lax.dynamic_slice_in_dim(seg_front, start_row + pad_rows, tok_rows)
    conv_seg = lax.dynamic_slice_in_dim(
        seg_front, start_row + pad_rows - tap_count + 1, tok_rows + tap_count - 1
    )
    key_seg = lax.dynamic_slice_in_dim(seg_front, start_row + tok_rows, window_blocks * tok_rows)
    prev_seg = conv_seg[tap_count - 2]
    pair_keep = (token_ids[:, None] >= token_ids[None, :]) & (own_seg[:, None] == own_seg[None, :])
    first_keep = (own_seg == prev_seg).astype(jnp.float32)
    last_keep = (own_seg == own_seg[-1]).astype(jnp.float32)
    conv_keeps = conv_masks(conv_seg, tap_count)
    key_pos = (
        start_row
        - (window_blocks - 1) * tok_rows
        + jnp.arange(window_blocks * tok_rows, dtype=jnp.int32)
    )
    attn_keep = (key_pos[None, :] <= positions[:, None]) & (key_seg[None, :] == own_seg[:, None])
    fetched = (
        lax.all_gather(w_zx, "seq", axis=0, tiled=True),
        lax.all_gather(w_bc, "seq", axis=0, tiled=True),
        lax.all_gather(w_dt, "seq", axis=0, tiled=True),
        lax.all_gather(w_mout, "seq", axis=1, tiled=True),
        lax.all_gather(w_q, "seq", axis=0, tiled=True),
        lax.all_gather(w_kv, "seq", axis=0, tiled=True),
        lax.all_gather(w_ao, "seq", axis=1, tiled=True),
        lax.all_gather(w_gu, "seq", axis=0, tiled=True),
        lax.all_gather(w_down, "seq", axis=1, tiled=True),
    )
    (
        zx_full,
        bc_full,
        dt_full,
        mout_full,
        query_full,
        keyval_full,
        attn_out_full,
        gateup_full,
        down_full,
    ) = fetched
    width = zx_full.shape[0]
    inner_half = zx_full.shape[2]
    ff_half = gateup_full.shape[2]
    x_float = x_in.astype(jnp.float32)
    norm_one = lax.rsqrt(jnp.mean(x_float * x_float, axis=-1, keepdims=True) + epsilon)
    normed = (x_float * norm_one * norm1_gain).astype(jnp.bfloat16)
    zx_proj = jnp.dot(
        normed, zx_full.reshape(width, 2 * inner_half), preferred_element_type=jnp.float32
    )
    gate_z = zx_proj[:, :inner_half]
    x_send = zx_proj[:, inner_half:].astype(jnp.bfloat16)
    bc_send = jnp.dot(normed, bc_full, preferred_element_type=jnp.float32).astype(jnp.bfloat16)
    dt_raw = jnp.dot(normed, dt_full, preferred_element_type=jnp.float32) + dt_bias
    edge_x, edge_bc = from_behind(
        (x_send[tok_rows - tap_count + 1 :], bc_send[tok_rows - tap_count + 1 :]), "seq", 1
    )
    ext_x = jnp.concatenate([edge_x, x_send], 0).astype(jnp.float32)
    ext_bc = jnp.concatenate([edge_bc, bc_send], 0).astype(jnp.float32)
    pre_x = conv_apply(ext_x, conv_keeps, conv_x)
    pre_bc = conv_apply(ext_bc, conv_keeps, conv_bc)
    conv_xs = jax.nn.silu(pre_x)
    conv_bcs = jax.nn.silu(pre_bc)
    b_matrix = conv_bcs[:, :NS]
    c_matrix = conv_bcs[:, NS:]
    step_size = jax.nn.softplus(dt_raw)
    rate = -jnp.exp2(-decay_exp.astype(jnp.float32)) * (256.0 / TOK_DEV)
    log_decay = step_size * rate[None, :]
    heads_here = log_decay.shape[1]
    zero_state = jnp.zeros((heads_here, MP, NS), jnp.float32)
    unit_carry = jnp.ones((heads_here,), jnp.float32)
    local_end, local_carry = ssd_end(
        conv_xs, b_matrix, log_decay, step_size, zero_state, first_keep, last_keep
    )
    _, state_in = entering(
        (local_carry, local_end), "seq", combine_affine, (unit_carry, zero_state), False
    )
    ssd_y = ssd_out(
        conv_xs, b_matrix, c_matrix, log_decay, step_size, state_in, skip_d, pair_keep, first_keep
    )
    silu_z = jax.nn.silu(gate_z)
    gated = ssd_y * silu_z
    square_part = jnp.sum(gated * gated, axis=-1)
    mamba_in = (gated * mnorm_gain).astype(jnp.bfloat16)
    mamba_part = jnp.dot(mamba_in, mout_full, preferred_element_type=jnp.float32)
    q_heads = query_full.shape[1] // AD
    query_raw = jnp.dot(normed, query_full, preferred_element_type=jnp.float32).reshape(
        tok_rows, q_heads, AD
    )
    keyval = jnp.dot(normed, keyval_full.reshape(width, 2 * AD), preferred_element_type=jnp.float32)
    query16 = rotate(query_raw, positions, 1.0).astype(jnp.bfloat16)
    key_rot = rotate(keyval[:, None, :AD] * key_multiplier, positions, 1.0)[:, 0, :]
    kv_send = jnp.concatenate([key_rot, keyval[:, AD:]], axis=-1).astype(jnp.bfloat16)
    reached = double_window(kv_send, reach_blocks, tok_rows)
    window_flat = jnp.concatenate(
        [jnp.zeros((lead_blocks * tok_rows, 2 * AD), jnp.bfloat16), reached], 0
    )
    attn_out16, log_sum = attend(query16, window_flat, attn_keep, group_rows, group_total)
    attn_flat = attn_out16.reshape(tok_rows, q_heads * AD)
    attn_part = jnp.dot(attn_flat, attn_out_full, preferred_element_type=jnp.float32)
    mamba_sum, attn_sum, square_sum = lax.psum((mamba_part, attn_part, square_part), "head")
    mamba_scale = lax.rsqrt(square_sum / MI + epsilon)[:, None]
    hidden_one = (
        x_float + mamba_multiplier * mamba_scale * mamba_sum + attention_multiplier * attn_sum
    )
    norm_two = lax.rsqrt(jnp.mean(hidden_one * hidden_one, axis=-1, keepdims=True) + epsilon)
    normed_two = (hidden_one * norm_two * norm2_gain).astype(jnp.bfloat16)
    gateup = jnp.dot(
        normed_two, gateup_full.reshape(width, 2 * ff_half), preferred_element_type=jnp.float32
    )
    gate_pre = gateup[:, :ff_half] * gate_multiplier
    up_proj = gateup[:, ff_half:]
    gate_act = jax.nn.silu(gate_pre)
    ff_hidden = (gate_act * up_proj).astype(jnp.bfloat16)
    ff_part = jnp.dot(ff_hidden, down_full, preferred_element_type=jnp.float32)
    ff_sum = lax.psum(ff_part.astype(jnp.bfloat16), "head").astype(jnp.float32)
    output = (hidden_one + down_multiplier * ff_sum).astype(jnp.bfloat16)
    (
        zx_back,
        bc_back,
        dt_back,
        mout_back,
        query_back,
        keyval_back,
        attn_out_back,
        gateup_back,
        down_back,
    ) = fetched
    grad_out = cotangent.astype(jnp.float32)
    grad_ff = (down_multiplier * grad_out).astype(jnp.bfloat16)
    grad_down = product_t(ff_hidden, grad_ff)
    grad_hidden = jnp.dot(grad_ff, down_back.T, preferred_element_type=jnp.float32)
    silu_slope = silu_grad(gate_pre)
    grad_gateup = jnp.concatenate(
        [grad_hidden * up_proj * silu_slope * gate_multiplier, grad_hidden * gate_act], axis=-1
    ).astype(jnp.bfloat16)
    grad_gu_weight = product_t(normed_two, grad_gateup).reshape(width, 2, ff_half)
    grad_two_part = jnp.dot(
        grad_gateup, gateup_back.reshape(width, 2 * ff_half).T, preferred_element_type=jnp.float32
    )
    grad_normed_two = lax.psum(grad_two_part, "head")
    scaled_two = grad_normed_two * norm2_gain
    grad_gain_two = jnp.sum(grad_normed_two * hidden_one * norm_two, axis=0)
    grad_hidden_one = (
        grad_out
        + norm_two * scaled_two
        - hidden_one * norm_two**3 * jnp.mean(scaled_two * hidden_one, axis=-1, keepdims=True)
    )
    grad_mamba16 = (mamba_multiplier * mamba_scale * grad_hidden_one).astype(jnp.bfloat16)
    grad_scale = mamba_multiplier * jnp.sum(grad_hidden_one * mamba_sum, axis=-1, keepdims=True)
    grad_mout = product_t(mamba_in, grad_mamba16)
    grad_mamba_in = jnp.dot(grad_mamba16, mout_back.T, preferred_element_type=jnp.float32)
    grad_mnorm = jnp.sum(grad_mamba_in * gated, axis=0)
    grad_gated = mnorm_gain * grad_mamba_in - grad_scale * mamba_scale**3 * gated / MI
    grad_ssd_y = grad_gated * silu_z
    grad_z = grad_gated * ssd_y * silu_grad(gate_z)

    def out_part(chan_in, b_in, c_in, log_in, step_in, state_given, skip_in):
        return ssd_out(
            chan_in, b_in, c_in, log_in, step_in, state_given, skip_in, pair_keep, first_keep
        )

    _, pull_out = jax.vjp(
        out_part, conv_xs, b_matrix, c_matrix, log_decay, step_size, state_in, skip_d
    )
    (
        grad_xs_one,
        grad_b_one,
        grad_c_one,
        grad_log_one,
        grad_step_one,
        grad_state_local,
        grad_skip,
    ) = pull_out(grad_ssd_y)
    _, grad_state_end = entering(
        (local_carry, grad_state_local), "seq", combine_affine, (unit_carry, zero_state), True
    )

    def end_part(chan_in, b_in, log_in, step_in):
        return ssd_end(chan_in, b_in, log_in, step_in, state_in, first_keep, last_keep)[0]

    _, pull_end = jax.vjp(end_part, conv_xs, b_matrix, log_decay, step_size)
    grad_xs_two, grad_b_two, grad_log_two, grad_step_two = pull_end(grad_state_end)
    grad_step = grad_step_one + grad_step_two + (grad_log_one + grad_log_two) * rate[None, :]
    grad_dt_raw = grad_step * jax.nn.sigmoid(dt_raw)
    grad_dt_bias = jnp.sum(grad_dt_raw, axis=0)
    grad_pre_x = (grad_xs_one + grad_xs_two) * silu_grad(pre_x)
    grad_pre_bc = jnp.concatenate([grad_b_one + grad_b_two, grad_c_one], axis=-1) * silu_grad(
        pre_bc
    )
    grad_ext_x, grad_conv_x = conv_grads(ext_x, conv_keeps, conv_x, grad_pre_x)
    grad_ext_bc, grad_conv_bc = conv_grads(ext_bc, conv_keeps, conv_bc, grad_pre_bc)
    back_x, back_bc = from_behind(
        (grad_ext_x[: tap_count - 1], grad_ext_bc[: tap_count - 1]), "seq", -1
    )
    grad_x_send = grad_ext_x[tap_count - 1 :].at[tok_rows - tap_count + 1 :].add(back_x)
    grad_bc_send = grad_ext_bc[tap_count - 1 :].at[tok_rows - tap_count + 1 :].add(back_bc)
    grad_zx16 = jnp.concatenate([grad_z, grad_x_send], axis=-1).astype(jnp.bfloat16)
    grad_bc16 = grad_bc_send.astype(jnp.bfloat16)
    grad_dt16 = grad_dt_raw.astype(jnp.bfloat16)
    grad_zx_weight = product_t(normed, grad_zx16).reshape(width, 2, inner_half)
    grad_bc_weight = product_t(normed, grad_bc16)
    grad_dt_weight = product_t(normed, grad_dt16)
    grad_normed = (
        jnp.dot(
            grad_zx16, zx_back.reshape(width, 2 * inner_half).T, preferred_element_type=jnp.float32
        )
        + jnp.dot(grad_bc16, bc_back.T, preferred_element_type=jnp.float32)
        + jnp.dot(grad_dt16, dt_back.T, preferred_element_type=jnp.float32)
    )
    grad_attn16 = (attention_multiplier * grad_hidden_one).astype(jnp.bfloat16)
    grad_attn_out = product_t(attn_flat, grad_attn16)
    grad_heads16 = (
        jnp.dot(grad_attn16, attn_out_back.T, preferred_element_type=jnp.float32)
        .astype(jnp.bfloat16)
        .reshape(tok_rows, q_heads, AD)
    )

    def back_group(group_index, carried):
        query_acc, window_grads = carried
        start = group_index * group_rows
        group_kv = lax.dynamic_slice_in_dim(window_flat, start, group_rows)
        group_mask = lax.dynamic_slice_in_dim(attn_keep, start, group_rows, 1)

        def back_live(unused):
            return attend_back(query16, group_kv, group_mask, log_sum, attn_out16, grad_heads16)

        def dead(unused):
            return (
                jnp.zeros((tok_rows, q_heads, AD), jnp.float32),
                jnp.zeros((group_rows, 2 * AD), jnp.float32),
            )

        part_query, part_window = lax.cond(jnp.any(group_mask), back_live, dead, 0)
        return (
            query_acc + part_query,
            lax.dynamic_update_slice_in_dim(window_grads, part_window, start, 0),
        )

    grad_query, grad_window = lax.fori_loop(
        0,
        group_total,
        back_group,
        (
            jnp.zeros((tok_rows, q_heads, AD), jnp.float32),
            jnp.zeros((window_blocks * tok_rows, 2 * AD), jnp.float32),
        ),
    )
    grad_kv_own = double_back(grad_window[lead_blocks * tok_rows :], reach_blocks, tok_rows)
    grad_q16 = (
        rotate(grad_query, positions, -1.0).reshape(tok_rows, q_heads * AD).astype(jnp.bfloat16)
    )
    grad_key = rotate(grad_kv_own[:, None, :AD], positions, -1.0)[:, 0, :] * key_multiplier
    grad_kv16 = jnp.concatenate([grad_key, grad_kv_own[:, AD:]], axis=-1).astype(jnp.bfloat16)
    grad_q_weight = product_t(normed, grad_q16)
    grad_kv_weight = product_t(normed, grad_kv16).reshape(width, 2, AD)
    grad_normed = (
        grad_normed
        + jnp.dot(grad_q16, query_back.T, preferred_element_type=jnp.float32)
        + jnp.dot(
            grad_kv16, keyval_back.reshape(width, 2 * AD).T, preferred_element_type=jnp.float32
        )
    )
    grad_normed_sum, grad_bc_summed, grad_conv_bc_summed = (
        lax.psum(grad_normed.astype(jnp.bfloat16), "head").astype(jnp.float32),
        lax.psum(grad_bc_weight.astype(jnp.bfloat16), "head").astype(jnp.float32),
        lax.psum(grad_conv_bc.astype(jnp.bfloat16), "head").astype(jnp.float32),
    )
    scaled_one = grad_normed_sum * norm1_gain
    grad_gain_one = jnp.sum(grad_normed_sum * x_float * norm_one, axis=0)
    x_grad = (
        grad_hidden_one
        + norm_one * scaled_one
        - x_float * norm_one**3 * jnp.mean(scaled_one * x_float, axis=-1, keepdims=True)
    )
    shard_zx, shard_bc, shard_dt, shard_mout, shard_q, shard_kv, shard_ao, shard_gu, shard_down = (
        lax.psum_scatter(grad_zx_weight, "seq", scatter_dimension=0, tiled=True),
        lax.psum_scatter(grad_bc_summed, "seq", scatter_dimension=0, tiled=True),
        lax.psum_scatter(grad_dt_weight, "seq", scatter_dimension=0, tiled=True),
        lax.psum_scatter(grad_mout, "seq", scatter_dimension=1, tiled=True),
        lax.psum_scatter(grad_q_weight, "seq", scatter_dimension=0, tiled=True),
        lax.psum_scatter(grad_kv_weight, "seq", scatter_dimension=0, tiled=True),
        lax.psum_scatter(grad_attn_out, "seq", scatter_dimension=1, tiled=True),
        lax.psum_scatter(grad_gu_weight, "seq", scatter_dimension=0, tiled=True),
        lax.psum_scatter(grad_down, "seq", scatter_dimension=1, tiled=True),
    )
    sum_gain_one, sum_gain_two, sum_mnorm, sum_conv_x, sum_conv_bc, sum_dt_bias, sum_skip = (
        lax.psum(
            (
                grad_gain_one,
                grad_gain_two,
                grad_mnorm,
                grad_conv_x,
                grad_conv_bc_summed,
                grad_dt_bias,
                grad_skip,
            ),
            "seq",
        )
    )
    return (
        output,
        x_grad,
        shard_zx,
        shard_bc,
        shard_dt,
        shard_mout,
        shard_q,
        shard_kv,
        shard_ao,
        shard_gu,
        shard_down,
        sum_gain_one,
        sum_gain_two,
        sum_mnorm,
        sum_conv_x,
        sum_conv_bc,
        sum_dt_bias,
        sum_skip,
    )


def solution(mesh):
    in_specs = (
        P("seq", None),
        P(),
        P("head"),
        P("seq", None),
        P("seq", None, "head"),
        P("seq", None),
        P("seq", "head"),
        P("head", "seq"),
        P("seq", "head"),
        P("seq", None, "head"),
        P("head", "seq"),
        P("seq", None, "head"),
        P("head", "seq"),
        P(),
        P(),
        P("head"),
        P(None, "head"),
        P(),
        P("head"),
        P("head"),
    )
    out_specs = (
        P("seq", None),
        P("seq", None),
        P("seq", None, "head"),
        P("seq", None),
        P("seq", "head"),
        P("head", "seq"),
        P("seq", "head"),
        P("seq", None, "head"),
        P("head", "seq"),
        P("seq", None, "head"),
        P("head", "seq"),
        P(),
        P(),
        P("head"),
        P(None, "head"),
        P(),
        P("head"),
        P("head"),
    )
    return jax.shard_map(local, mesh=mesh, in_specs=in_specs, out_specs=out_specs, check_vma=False)
```

profile of v0, /device:TPU:0, one launch (start us, length us, event | category | flops | bytes accessed | tf_op | source)
XLA Modules:
  0.0 1723.9 jit_solution(8831426849737699667)
XLA Ops:
  9.8 46.5 %all_gather.47 = bf16[1024,256]{1,0:T(8,128)(2,1)S(1)} all-gather(bf16[64,256]{1,0:T(8,128)(2,1)} %param.75), channel_id=1, replica_groups=mesh['seq'=16,'head'=2] {'seq'}, dimensions={0}, use_global_device_ids=true | all-gather | bytes 557056 | tf_op jit(solution)/shard_map/all_gather | solution.py:312
  62.3 36.3 %all-gather.2 = bf16[16,64,12]{1,2,0:T(8,128)(2,1)S(1)} all-gather(bf16[1,64,12]{1,2,0:T(8,128)(2,1)S(1)} %bitcast.248), channel_id=1, replica_groups=mesh['seq'=16,'head'=2] {'seq'}, dimensions={0}, use_global_device_ids=true | all-gather | bytes 26112 | tf_op jit(solution)/shard_map/all_gather | solution.py:313
  116.6 43.8 %all_gather.52 = bf16[1024,2,64]{2,1,0:T(2,128)(2,1)S(1)} all-gather(bf16[64,2,64]{2,1,0:T(2,128)(2,1)S(1)} %copy-done.91), channel_id=1, replica_groups=mesh['seq'=16,'head'=2] {'seq'}, dimensions={0}, use_global_device_ids=true | all-gather | bytes 278528 | tf_op jit(solution)/shard_map/all_gather | solution.py:316
  164.2 43.4 %all_gather.53 = bf16[1024,256]{1,0:T(8,128)(2,1)S(1)} all-gather(bf16[64,256]{1,0:T(8,128)(2,1)S(1)} %copy-done.92), channel_id=1, replica_groups=mesh['seq'=16,'head'=2] {'seq'}, dimensions={0}, use_global_device_ids=true | all-gather | bytes 557056 | tf_op jit(solution)/shard_map/all_gather | solution.py:315
  207.6 44.1 %all_gather.54 = bf16[256,1024]{0,1:T(8,128)(2,1)} all-gather(bf16[256,64]{0,1:T(8,128)(2,1)S(1)} %copy-done.93), channel_id=1, replica_groups=mesh['seq'=16,'head'=2] {'seq'}, dimensions={1}, use_global_device_ids=true | all-gather | bytes 557056 | tf_op jit(solution)/shard_map/all_gather | solution.py:317
  252.7 37.6 %all-gather.3 = f32[16,1,12]{2,1,0:T(1,128)} all-gather(f32[1,1,12]{2,1,0:T(1,128)S(1)} %bitcast.253), channel_id=1, replica_groups=mesh['seq'=16,'head'=2] {'seq'}, dimensions={0}, use_global_device_ids=true | all-gather | bytes 816 | tf_op jit(solution)/shard_map/all_gather | solution.py:35
  319.8 9.1 while.92
  346.4 13.5 all-gather.15.cloned.1.call-done
  368.1 41.3 %all-reduce.20.cloned.1.call-done = (f32[176,1024]{1,0:T(8,128)}, f32[176,1024]{1,0:T(8,128)}) async-done(((f32[176,1024]{1,0:T(8,128)}, f32[176,1024]{1,0:T(8,128)}), (f32[176,1024]{1,0:T(8,128)}, f32[176,1024]{1,0:T(8,128)})) %all-reduce.20.cloned.1.call-update) | async-done | bytes 1441808 | tf_op jit(solution)/shard_map/psum | solution.py:391
  415.7 57.9 %all-gather.17.cloned.1.call-done = bf16[1024,1024]{0,1:T(8,128)(2,1)} async-done(((bf16[1024,64]{0,1:T(8,128)(2,1)}), bf16[1024,1024]{0,1:T(8,128)(2,1)}) %all-gather.17.cloned.1.call-update) | async-done | bytes 2097168 | tf_op jit(solution)/shard_map/all_gather | solution.py:319
  480.6 17.8 %all-reduce.16.cloned.1.call-done = f32[176,1024]{1,0:T(8,128)} async-done(((f32[176,1024]{1,0:T(8,128)}), f32[176,1024]{1,0:T(8,128)}) %all-reduce.16.cloned.1.call-update) | async-done | bytes 720912 | tf_op jit(solution)/shard_map/psum | solution.py:431
  516.4 35.4 %while.94 = (s32[]{:T(128)}, f32[176,4,64]{0,2,1:T(8,128)}, f32[2816,128]{0,1:T(8,128)}, pred[176,2816]{1,0:T(8,128)(4,1)S(1)}, bf16[2816,128]{0,1:T(8,128)(2,1)...) while((s32[]{:T(128)}, f32[176,4,64]{0,2,1:T(8,128)}, ...), condition=%wide.region_39.40_spmd.clone, body=%wide.region_34.39_spmd.clone.sunk | while | flops 322724160 | bytes 13295451 | solution.py:530
  566.0 29.4 %collective-permute-done.8 = bf16[880,128]{0,1:T(8,128)(2,1)S(1)} collective-permute-done((bf16[880,128]{0,1:T(8,128)(2,1)S(1)}, bf16[880,128]{0,1:T(8,128)(2,1)S(1)}, u32[]{:S(2)}, u32[]{:S(2)}) %collective-permute-start.8) | collective-permute-done | bytes 225312 | tf_op jit(solution)/shard_map/ppermute | solution.py:28
  604.7 8.4 collective-permute-done.9
  629.0 27.4 %while.93 = (s32[]{:T(128)}, f32[12,64,128]{2,1,0:T(8,128)S(1)}, s32[]{:T(128)}, f32[16,12]{1,0:T(8,128)}, f32[16,12,64,128]{3,2,1,0:T(8,128)}, /*index=5*/s32[]{:T(128)}, s32[]{:T(128)}, s32[]{:T(128)}, s32[]{:T(128)}) while((s32[]{:T(128)}, f32[12,64,128]{2,1,0:T(8,128)S(1)}, s32[]{:T(128)}, f32[16,12]{1,0:T(8,128)}, ...), condition=%wide.region_25.26_spmd, body=%wide.region_24.25_spmd.sunk | while | flops 196614 | bytes 1179947 | solution.py:44
  715.4 11.8 reshape.741
  758.3 54.4 %reduce-scatter.19.cloned.1.call-done = f32[64,12]{1,0:T(8,128)} async-done(((f32[1024,12]{1,0:T(8,128)}), f32[64,12]{1,0:T(8,128)}) %reduce-scatter.19.cloned.1.call-update) | async-done | bytes 3088
  814.4 77.0 %all-reduce.7 = (f32[1024]{0:T(1024)}, f32[1024]{0:T(1024)}, f32[768]{0:T(1024)}, f32[4,768]{1,0:T(4,128)}, f32[4,256]{1,0:T(4,128)}, /*index=5*/f32[12]{0:T(128)}, f32[12]{0:T(128)}) all-reduce(f32[1024]{0:T(1024)S(1)} %get-tuple-element.939, f32[1024]{0:T(1024)S(1)} %copy-done.105, ...), channel_id=1, replica_groups=mesh['seq'=16,'head'=2] {'seq'}, use_global_device_ids=true, to_apply=%region_53.54 | all-reduce | flops 6936 | bytes 53440 | tf_op jit(solution)/shard_map/psum | solution.py:578
  893.3 353.5 %all-reduce.18.cloned.1.call-done = (f32[1024,2,768]{2,1,0:T(2,128)}, f32[1024,2,64]{2,1,0:T(2,128)}, f32[1024,2,1024]{2,1,0:T(2,128)}) async-done(((f32[1024,2,768]{2,1,0:T(2,128)}, f32[1024,2,64]{2,1,0:T(2,128)}, f32[1024,2,1024]{2,1,0:T(2,128)}), (f32[1024,2,768]{2,1,0:T(2,128)}, f32[1024,2,64]{2,1,0:T(2,128)}, f32[1024,2,1024]{2,1,0:T(2,128)})) %all-reduce.18.cloned.1.call-update) | async-done | bytes 15204368
  1252.0 75.4 %reduce-scatter.13.cloned.1.call-done = f32[64,256]{1,0:T(8,128)} async-done(((f32[1024,256]{1,0:T(8,128)}), f32[64,256]{1,0:T(8,128)}) %reduce-scatter.13.cloned.1.call-update) | async-done | bytes 65552 | tf_op jit(solution)/shard_map/reduce_scatter | solution.py:571
  1327.3 77.9 %reduce-scatter.15.cloned.1.call-done = f32[256,64]{0,1:T(8,128)} async-done(((f32[256,1024]{0,1:T(8,128)}), f32[256,64]{0,1:T(8,128)}) %reduce-scatter.15.cloned.1.call-update) | async-done | bytes 65552 | tf_op jit(solution)/shard_map/reduce_scatter | solution.py:573
  1405.2 133.8 %reduce-scatter.11.cloned.1.call-done = f32[768,64]{0,1:T(8,128)} async-done(((f32[768,1024]{0,1:T(8,128)}), f32[768,64]{0,1:T(8,128)}) %reduce-scatter.11.cloned.1.call-update) | async-done | bytes 196624 | tf_op jit(solution)/shard_map/reduce_scatter | solution.py:570
  1539.0 97.0 %reduce-scatter.17.cloned.1.call-done = f32[1024,64]{0,1:T(8,128)} async-done(((f32[1024,1024]{0,1:T(8,128)}), f32[1024,64]{0,1:T(8,128)}) %reduce-scatter.17.cloned.1.call-update) | async-done | bytes 262160 | tf_op jit(solution)/shard_map/reduce_scatter | solution.py:575
  1635.9 81.0 %reduce-scatter.9.cloned.1.call-done = f32[64,256]{1,0:T(8,128)} async-done(((f32[1024,256]{1,0:T(8,128)}), f32[64,256]{1,0:T(8,128)}) %reduce-scatter.9.cloned.1.call-update) | async-done | bytes 65552 | tf_op jit(solution)/shard_map/reduce_scatter | solution.py:568
  (624 shorter events, 335.6 us)
Async XLA Ops:
  7.3 95.1 %all-gather.11.cloned.1.call-start = ((), (), s32[]{:S(2)}) async-start(), calls=%async_computation.6 | async-start | bytes 3342336 | tf_op jit(solution)/shard_map/all_gather | solution.py:311
  8.0 324.4 %all-gather.19.cloned.1.call-start = ((), (), s32[]{:S(2)}) async-start(), calls=%async_computation.16 | async-start | bytes 6684672 | tf_op jit(solution)/shard_map/all_gather | solution.py:35
  58.4 43.9 %collective-permute-start.1 = (bf16[3,256]{1,0:T(4,128)(2,1)S(1)}, bf16[3,256]{1,0:T(4,128)(2,1)S(1)}, u32[]{:S(2)}, u32[]{:S(2)}) collective-permute-start(bf16[3,256]{1,0:T(4,128)(2,1)S(1)} %slice.531), channel_id=1, source_target_pairs={{0,2},{2,4},{4,6},{6,8},{8,10},{10,12},{12,14},{14,16},{16,18},{18... | collective-permute-start | bytes 4616 | tf_op jit(solution)/shard_map/ppermute | solution.py:28
  115.2 227.3 %all-gather.13.cloned.1.call-start = ((), (), s32[]{:S(2)}) async-start(), calls=%async_computation.7 | async-start | bytes 1671168 | tf_op jit(solution)/shard_map/all_gather | solution.py:314
  115.9 243.9 %all-gather.15.cloned.1.call-start = ((), (), s32[]{:S(2)}) async-start(), calls=%async_computation.8 | async-start | bytes 4456448 | tf_op jit(solution)/shard_map/all_gather | solution.py:318
  116.5 292.9 %all-reduce.20.cloned.1.call-start = ((), (), s32[]{:S(2)}) async-start(), calls=%async_computation.20 | async-start | bytes 2883584 | tf_op jit(solution)/shard_map/psum | solution.py:391
  161.5 128.7 %collective-permute-start.2 = (bf16[176,128]{0,1:T(8,128)(2,1)S(1)}, bf16[176,128]{0,1:T(8,128)(2,1)S(1)}, u32[]{:S(2)}, u32[]{:S(2)}) collective-permute-start(bf16[176,128]{0,1:T(8,128)(2,1)S(1)} %pad_maximum_fusion.9), channel_id=1, source_target_pairs={{0,2},{2,4},{4,6},{6,8},{8,10},{10,12},{12,14},{14,16},{16,18},{18... | collective-permute-start | bytes 135176 | tf_op jit(solution)/shard_map/ppermute | solution.py:28
  302.4 6.8 collective-permute-start.5
  345.7 127.9 %all-gather.17.cloned.1.call-start = ((), (), s32[]{:S(2)}) async-start(), calls=%async_computation.9 | async-start | bytes 2228224 | tf_op jit(solution)/shard_map/all_gather | solution.py:319
  346.3 152.0 %all-reduce.16.cloned.1.call-start = ((), (), s32[]{:S(2)}) async-start(), calls=%async_computation.10 | async-start | bytes 1441792 | tf_op jit(solution)/shard_map/psum | solution.py:431
  480.5 148.4 %all-gather.21.cloned.1.call-start = ((), (), s32[]{:S(2)}) async-start(), calls=%async_computation.17 | async-start | bytes 6684672 | tf_op jit(solution)/shard_map/all_gather | solution.py:35
  511.2 240.7 %all-reduce.22.cloned.1.call-start = ((), (), s32[]{:S(2)}) async-start(), calls=%async_computation.21 | async-start | bytes 2490368 | tf_op jit(solution)/shard_map/psum | solution.py:406
  554.9 40.5 %collective-permute-start.8 = (bf16[880,128]{0,1:T(8,128)(2,1)S(1)}, bf16[880,128]{0,1:T(8,128)(2,1)S(1)}, u32[]{:S(2)}, u32[]{:S(2)}) collective-permute-start(bf16[880,128]{0,1:T(8,128)(2,1)S(1)} %slice.679), channel_id=1, source_target_pairs={{16,0},{18,2},{20,4},{22,6},{24,8},{26,10},{28,12},{30,14},{17,1},... | collective-permute-start | bytes 675848 | tf_op jit(solution)/shard_map/ppermute | solution.py:28
  601.5 11.6 collective-permute-start.9
  614.3 6.5 collective-permute-start.10
  688.4 8.9 collective-permute-start.7
  692.6 9.5 collective-permute-start.6
  710.6 102.0 %reduce-scatter.19.cloned.1.call-start = ((), (), s32[]{:S(2)}) async-start(), calls=%async_computation.18 | async-start | bytes 557056
  730.1 516.8 %all-reduce.18.cloned.1.call-start = ((), (), s32[]{:S(2)}) async-start(), calls=%async_computation.19 | async-start | bytes 31457280
  742.4 584.9 %reduce-scatter.13.cloned.1.call-start = ((), (), s32[]{:S(2)}) async-start(), calls=%async_computation.13 | async-start | bytes 1114112 | tf_op jit(solution)/shard_map/reduce_scatter | solution.py:571
  743.9 661.3 %reduce-scatter.15.cloned.1.call-start = ((), (), s32[]{:S(2)}) async-start(), calls=%async_computation.14 | async-start | bytes 1114112 | tf_op jit(solution)/shard_map/reduce_scatter | solution.py:573
  745.4 793.5 %reduce-scatter.11.cloned.1.call-start = ((), (), s32[]{:S(2)}) async-start(), calls=%async_computation.12 | async-start | bytes 3342336 | tf_op jit(solution)/shard_map/reduce_scatter | solution.py:570
  747.9 888.1 %reduce-scatter.17.cloned.1.call-start = ((), (), s32[]{:S(2)}) async-start(), calls=%async_computation.15 | async-start | bytes 4456448 | tf_op jit(solution)/shard_map/reduce_scatter | solution.py:575
  751.8 965.1 %reduce-scatter.9.cloned.1.call-start = ((), (), s32[]{:S(2)}) async-start(), calls=%async_computation.11 | async-start | bytes 1114112 | tf_op jit(solution)/shard_map/reduce_scatter | solution.py:568
  (153 other events, 3861.5 us)
Sparse Core Ops, SparseCore 0:
  10.9 71.9 all-gather.10
  115.3 103.9 all-gather.18
  222.1 58.7 all-gather.12
  283.4 76.3 all-gather.14
  362.7 46.6 all-reduce.19
  412.0 61.5 all-gather.16
  480.6 17.6 all-reduce.15
  511.3 105.9 all-gather.20
  710.7 20.4 all-reduce.21
  733.9 78.7 reduce-scatter.18
  819.1 427.7 all-reduce.17
  1249.5 77.7 reduce-scatter.12
  1330.2 74.9 reduce-scatter.14
  1410.6 128.3 reduce-scatter.10
  1541.7 94.2 reduce-scatter.16
  1638.6 78.2 reduce-scatter.8
where the time goes:
time: 1740 us; the launch traced here: 1720 us
  waiting for transfers between devices  1060 us (61%)
  blocking collectives  334 us (19%)
  local copies, waits for them, and re-layouts  100 us (6%)
  matrix products  96.1 us (6%)
  other arithmetic  82.9 us (5%)
  starting transfers between devices  21.6 us (1%)
    unnamed x18, waiting for transfers between devices  411 us
    reduce_scatter x1, waiting for transfers between devices, local(): lax.psum_scatter(grad_mout, 'seq', scatter_dimension=1, tiled=True)  134 us
    reduce_scatter x1, waiting for transfers between devices, local(): lax.psum_scatter(grad_down, 'seq', scatter_dimension=1, tiled=True)  97 us
    reduce_scatter x1, waiting for transfers between devices, local(): lax.psum_scatter(grad_bc_summed, 'seq', scatter_dimension=0, tiled=True)  81 us
    reduce_scatter x1, waiting for transfers between devices, local(): lax.psum_scatter(grad_attn_out, 'seq', scatter_dimension=1, tiled=True)  77.9 us
    psum x1, blocking collectives, local(): lax.psum((grad_gain_one, grad_gain_two, grad_mnorm, grad_conv_x, grad_con...  77 us
    reduce_scatter x1, waiting for transfers between devices, local(): lax.psum_scatter(grad_q_weight, 'seq', scatter_dimension=0, tiled=True)  75.4 us
    all_gather x1, waiting for transfers between devices, local(): lax.all_gather(w_down, 'seq', axis=1, tiled=True)  57.9 us
  transfers between devices with their start and end apart: 28, of which 19 were waited for; matrix products, arithmetic and copies ran while one was open for 11% of the time, Pallas kernels for 0%

commit v1 on v0

--- a/solution.py
+++ b/solution.py
@@ -28,20 +28,46 @@
     return lax.ppermute(block, axis, route)
 
 
-def entering(part, axis, combine, identity, reverse):
-    count = lax.axis_size(axis)
-    place = lax.axis_index(axis)
+def gather_states(carry, end):
+    heads = end.shape[0]
+    packed = jnp.concatenate(
+        [end.reshape(heads, -1), jnp.broadcast_to(carry[:, None], (heads, end.shape[2]))], axis=1
+    )
+    gathered = lax.all_gather(packed, "seq")
+    ends = gathered[:, :, : end.shape[1] * end.shape[2]].reshape((-1,) + end.shape)
+    return (gathered[:, :, -1], ends)
+
+
+def entering(carries, ends, reverse):
+    count = lax.axis_size("seq")
+    place = lax.axis_index("seq")
     ahead = count - 1 - place if reverse else place
-    gathered = jax.tree.map(lambda a: lax.all_gather(a, axis), part)
-    state = jax.tree.map(lambda a, e: jnp.zeros_like(a) + jnp.asarray(e, a.dtype), part, identity)
-
-    def one(hop, state):
-        source = count - 1 - hop if reverse else hop
-        return combine(
-            state, jax.tree.map(lambda a: lax.dynamic_index_in_dim(a, source, 0, False), gathered)
-        )
-
-    return lax.fori_loop(0, ahead, one, state)
+    if reverse:
+        carries, ends = (carries[::-1], ends[::-1])
+    hops = jnp.arange(count, dtype=jnp.int32)
+    between = (hops[None, :] > hops[:, None]) & (hops[None, :] < ahead)
+    weights = jnp.prod(jnp.where(between[:, :, None], carries[None], 1.0), axis=1)
+    weights = jnp.where((hops < ahead)[:, None], weights, 0.0)
+    return jnp.sum(weights[:, :, None, None] * ends, axis=0)
+
+
+def head_sum(part):
+    count = lax.axis_size("head")
+    total = part.astype(jnp.float32)
+    if count != 2:
+        return lax.psum(total, "head")
+    return total + lax.ppermute(part, "head", [(0, 1), (1, 0)]).astype(jnp.float32)
+
+
+def seq_sum(part):
+    count = lax.axis_size("seq")
+    if count & (count - 1):
+        return lax.psum(part, "seq")
+    distance = 1
+    while distance < count:
+        part = part + lax.ppermute(part, "seq", [(i, i ^ distance) for i in range(count)])
+        distance = distance * 2
+    return part
 
 
 def silu_grad(values):
@@ -139,10 +165,6 @@
     return (end_state + carry_factor[:, None, None] * state_in, carry_factor)
 
 
-def combine_affine(earlier, later):
-    return (earlier[0] * later[0], later[0][:, None, None] * earlier[1] + later[1])
-
-
 def step_plan(reach_blocks):
     plan_list = []
     held_blocks = 1
@@ -249,6 +271,22 @@
         "gtk,tgd->kd", probs_rounded, grad_rows, preferred_element_type=jnp.float32
     )
     return (grad_query, jnp.concatenate([grad_keys, grad_values], axis=-1))
+
+
+def column_ends(parts):
+    ends = []
+    for part in parts[:-1]:
+        ends.append(part.shape[1] + (ends[-1] if ends else 0))
+    return ends
+
+
+def times_rows(left, right):
+    return jnp.einsum("tc,dc->td", left, right, preferred_element_type=jnp.float32)
+
+
+def scatter_sum(parts):
+    packed = jnp.concatenate([part.astype(jnp.bfloat16) for part in parts], axis=1)
+    return lax.psum_scatter(packed, "seq", scatter_dimension=0, tiled=True).astype(jnp.float32)
 
 
 def product_t(left, right):
@@ -307,41 +345,31 @@
         + jnp.arange(window_blocks * tok_rows, dtype=jnp.int32)
     )
     attn_keep = (key_pos[None, :] <= positions[:, None]) & (key_seg[None, :] == own_seg[:, None])
-    fetched = (
-        lax.all_gather(w_zx, "seq", axis=0, tiled=True),
-        lax.all_gather(w_bc, "seq", axis=0, tiled=True),
-        lax.all_gather(w_dt, "seq", axis=0, tiled=True),
-        lax.all_gather(w_mout, "seq", axis=1, tiled=True),
-        lax.all_gather(w_q, "seq", axis=0, tiled=True),
-        lax.all_gather(w_kv, "seq", axis=0, tiled=True),
-        lax.all_gather(w_ao, "seq", axis=1, tiled=True),
-        lax.all_gather(w_gu, "seq", axis=0, tiled=True),
-        lax.all_gather(w_down, "seq", axis=1, tiled=True),
-    )
-    (
-        zx_full,
-        bc_full,
-        dt_full,
-        mout_full,
-        query_full,
-        keyval_full,
-        attn_out_full,
-        gateup_full,
-        down_full,
-    ) = fetched
-    width = zx_full.shape[0]
-    inner_half = zx_full.shape[2]
-    ff_half = gateup_full.shape[2]
+    shard_rows, _, inner_half = w_zx.shape
+    ff_half = w_gu.shape[2]
+    heads_here = w_dt.shape[1]
+    width = x_in.shape[1]
+    q_width = w_q.shape[1]
+    in_parts = (w_zx.reshape(shard_rows, -1), w_bc, w_q, w_kv.reshape(shard_rows, -1), w_dt)
+    out_parts = (w_mout.T, w_ao.T)
+    ff_parts = (w_gu.reshape(shard_rows, -1), w_down.T)
+    in_full, out_full, ff_full = [
+        lax.all_gather(jnp.concatenate(parts, axis=1), "seq", axis=0, tiled=True)
+        for parts in (in_parts, out_parts, ff_parts)
+    ]
+    in_ends = column_ends(in_parts)
+    mout_full, attn_out_full = jnp.split(out_full, column_ends(out_parts), axis=1)
+    gateup_full, down_full = jnp.split(ff_full, column_ends(ff_parts), axis=1)
     x_float = x_in.astype(jnp.float32)
     norm_one = lax.rsqrt(jnp.mean(x_float * x_float, axis=-1, keepdims=True) + epsilon)
     normed = (x_float * norm_one * norm1_gain).astype(jnp.bfloat16)
-    zx_proj = jnp.dot(
-        normed, zx_full.reshape(width, 2 * inner_half), preferred_element_type=jnp.float32
+    zx_proj, bc_proj, q_proj, keyval, dt_proj = jnp.split(
+        jnp.dot(normed, in_full, preferred_element_type=jnp.float32), in_ends, axis=1
     )
     gate_z = zx_proj[:, :inner_half]
     x_send = zx_proj[:, inner_half:].astype(jnp.bfloat16)
-    bc_send = jnp.dot(normed, bc_full, preferred_element_type=jnp.float32).astype(jnp.bfloat16)
-    dt_raw = jnp.dot(normed, dt_full, preferred_element_type=jnp.float32) + dt_bias
+    bc_send = bc_proj.astype(jnp.bfloat16)
+    dt_raw = dt_proj + dt_bias
     edge_x, edge_bc = from_behind(
         (x_send[tok_rows - tap_count + 1 :], bc_send[tok_rows - tap_count + 1 :]), "seq", 1
     )
@@ -356,15 +384,12 @@
     step_size = jax.nn.softplus(dt_raw)
     rate = -jnp.exp2(-decay_exp.astype(jnp.float32)) * (256.0 / TOK_DEV)
     log_decay = step_size * rate[None, :]
-    heads_here = log_decay.shape[1]
     zero_state = jnp.zeros((heads_here, MP, NS), jnp.float32)
-    unit_carry = jnp.ones((heads_here,), jnp.float32)
     local_end, local_carry = ssd_end(
         conv_xs, b_matrix, log_decay, step_size, zero_state, first_keep, last_keep
     )
-    _, state_in = entering(
-        (local_carry, local_end), "seq", combine_affine, (unit_carry, zero_state), False
-    )
+    carries, ends = gather_states(local_carry, local_end)
+    state_in = entering(carries, ends, False)
     ssd_y = ssd_out(
         conv_xs, b_matrix, c_matrix, log_decay, step_size, state_in, skip_d, pair_keep, first_keep
     )
@@ -372,12 +397,9 @@
     gated = ssd_y * silu_z
     square_part = jnp.sum(gated * gated, axis=-1)
     mamba_in = (gated * mnorm_gain).astype(jnp.bfloat16)
-    mamba_part = jnp.dot(mamba_in, mout_full, preferred_element_type=jnp.float32)
-    q_heads = query_full.shape[1] // AD
-    query_raw = jnp.dot(normed, query_full, preferred_element_type=jnp.float32).reshape(
-        tok_rows, q_heads, AD
-    )
-    keyval = jnp.dot(normed, keyval_full.reshape(width, 2 * AD), preferred_element_type=jnp.float32)
+    mamba_part = times_rows(mamba_in, mout_full)
+    q_heads = q_width // AD
+    query_raw = q_proj.reshape(tok_rows, q_heads, AD)
     query16 = rotate(query_raw, positions, 1.0).astype(jnp.bfloat16)
     key_rot = rotate(keyval[:, None, :AD] * key_multiplier, positions, 1.0)[:, 0, :]
     kv_send = jnp.concatenate([key_rot, keyval[:, AD:]], axis=-1).astype(jnp.bfloat16)
@@ -387,48 +409,36 @@
     )
     attn_out16, log_sum = attend(query16, window_flat, attn_keep, group_rows, group_total)
     attn_flat = attn_out16.reshape(tok_rows, q_heads * AD)
-    attn_part = jnp.dot(attn_flat, attn_out_full, preferred_element_type=jnp.float32)
-    mamba_sum, attn_sum, square_sum = lax.psum((mamba_part, attn_part, square_part), "head")
+    attn_part = times_rows(attn_flat, attn_out_full)
+    square_sum = head_sum(square_part)
+    mamba_sum = head_sum(mamba_part)
+    attn_sum = head_sum(attn_part)
     mamba_scale = lax.rsqrt(square_sum / MI + epsilon)[:, None]
     hidden_one = (
         x_float + mamba_multiplier * mamba_scale * mamba_sum + attention_multiplier * attn_sum
     )
     norm_two = lax.rsqrt(jnp.mean(hidden_one * hidden_one, axis=-1, keepdims=True) + epsilon)
     normed_two = (hidden_one * norm_two * norm2_gain).astype(jnp.bfloat16)
-    gateup = jnp.dot(
-        normed_two, gateup_full.reshape(width, 2 * ff_half), preferred_element_type=jnp.float32
-    )
+    gateup = jnp.dot(normed_two, gateup_full, preferred_element_type=jnp.float32)
     gate_pre = gateup[:, :ff_half] * gate_multiplier
     up_proj = gateup[:, ff_half:]
     gate_act = jax.nn.silu(gate_pre)
     ff_hidden = (gate_act * up_proj).astype(jnp.bfloat16)
-    ff_part = jnp.dot(ff_hidden, down_full, preferred_element_type=jnp.float32)
-    ff_sum = lax.psum(ff_part.astype(jnp.bfloat16), "head").astype(jnp.float32)
+    ff_part = times_rows(ff_hidden, down_full)
+    ff_sum = head_sum(ff_part.astype(jnp.bfloat16))
     output = (hidden_one + down_multiplier * ff_sum).astype(jnp.bfloat16)
-    (
-        zx_back,
-        bc_back,
-        dt_back,
-        mout_back,
-        query_back,
-        keyval_back,
-        attn_out_back,
-        gateup_back,
-        down_back,
-    ) = fetched
     grad_out = cotangent.astype(jnp.float32)
     grad_ff = (down_multiplier * grad_out).astype(jnp.bfloat16)
-    grad_down = product_t(ff_hidden, grad_ff)
-    grad_hidden = jnp.dot(grad_ff, down_back.T, preferred_element_type=jnp.float32)
+    grad_hidden = jnp.dot(grad_ff, down_full, preferred_element_type=jnp.float32)
     silu_slope = silu_grad(gate_pre)
     grad_gateup = jnp.concatenate(
         [grad_hidden * up_proj * silu_slope * gate_multiplier, grad_hidden * gate_act], axis=-1
     ).astype(jnp.bfloat16)
-    grad_gu_weight = product_t(normed_two, grad_gateup).reshape(width, 2, ff_half)
-    grad_two_part = jnp.dot(
-        grad_gateup, gateup_back.reshape(width, 2 * ff_half).T, preferred_element_type=jnp.float32
-    )
-    grad_normed_two = lax.psum(grad_two_part, "head")
+    grad_two_part = times_rows(grad_gateup, gateup_full)
+    grad_normed_two = head_sum(grad_two_part)
+    ff_shard = scatter_sum((product_t(normed_two, grad_gateup), product_t(grad_ff, ff_hidden)))
+    shard_gu = ff_shard[:, : 2 * ff_half].reshape(shard_rows, 2, ff_half)
+    shard_down = ff_shard[:, 2 * ff_half :].T
     scaled_two = grad_normed_two * norm2_gain
     grad_gain_two = jnp.sum(grad_normed_two * hidden_one * norm_two, axis=0)
     grad_hidden_one = (
@@ -438,8 +448,11 @@
     )
     grad_mamba16 = (mamba_multiplier * mamba_scale * grad_hidden_one).astype(jnp.bfloat16)
     grad_scale = mamba_multiplier * jnp.sum(grad_hidden_one * mamba_sum, axis=-1, keepdims=True)
-    grad_mout = product_t(mamba_in, grad_mamba16)
-    grad_mamba_in = jnp.dot(grad_mamba16, mout_back.T, preferred_element_type=jnp.float32)
+    grad_attn16 = (attention_multiplier * grad_hidden_one).astype(jnp.bfloat16)
+    out_shard = scatter_sum((product_t(grad_mamba16, mamba_in), product_t(grad_attn16, attn_flat)))
+    shard_mout = out_shard[:, :inner_half].T
+    shard_ao = out_shard[:, inner_half:].T
+    grad_mamba_in = jnp.dot(grad_mamba16, mout_full, preferred_element_type=jnp.float32)
     grad_mnorm = jnp.sum(grad_mamba_in * gated, axis=0)
     grad_gated = mnorm_gain * grad_mamba_in - grad_scale * mamba_scale**3 * gated / MI
     grad_ssd_y = grad_gated * silu_z
@@ -462,9 +475,7 @@
         grad_state_local,
         grad_skip,
     ) = pull_out(grad_ssd_y)
-    _, grad_state_end = entering(
-        (local_carry, grad_state_local), "seq", combine_affine, (unit_carry, zero_state), True
-    )
+    grad_state_end = entering(carries, lax.all_gather(grad_state_local, "seq"), True)
 
     def end_part(chan_in, b_in, log_in, step_in):
         return ssd_end(chan_in, b_in, log_in, step_in, state_in, first_keep, last_keep)[0]
@@ -488,20 +499,8 @@
     grad_zx16 = jnp.concatenate([grad_z, grad_x_send], axis=-1).astype(jnp.bfloat16)
     grad_bc16 = grad_bc_send.astype(jnp.bfloat16)
     grad_dt16 = grad_dt_raw.astype(jnp.bfloat16)
-    grad_zx_weight = product_t(normed, grad_zx16).reshape(width, 2, inner_half)
-    grad_bc_weight = product_t(normed, grad_bc16)
-    grad_dt_weight = product_t(normed, grad_dt16)
-    grad_normed = (
-        jnp.dot(
-            grad_zx16, zx_back.reshape(width, 2 * inner_half).T, preferred_element_type=jnp.float32
-        )
-        + jnp.dot(grad_bc16, bc_back.T, preferred_element_type=jnp.float32)
-        + jnp.dot(grad_dt16, dt_back.T, preferred_element_type=jnp.float32)
-    )
-    grad_attn16 = (attention_multiplier * grad_hidden_one).astype(jnp.bfloat16)
-    grad_attn_out = product_t(attn_flat, grad_attn16)
     grad_heads16 = (
-        jnp.dot(grad_attn16, attn_out_back.T, preferred_element_type=jnp.float32)
+        jnp.dot(grad_attn16, attn_out_full, preferred_element_type=jnp.float32)
         .astype(jnp.bfloat16)
         .reshape(tok_rows, q_heads, AD)
     )
@@ -542,20 +541,13 @@
     )
     grad_key = rotate(grad_kv_own[:, None, :AD], positions, -1.0)[:, 0, :] * key_multiplier
     grad_kv16 = jnp.concatenate([grad_key, grad_kv_own[:, AD:]], axis=-1).astype(jnp.bfloat16)
-    grad_q_weight = product_t(normed, grad_q16)
-    grad_kv_weight = product_t(normed, grad_kv16).reshape(width, 2, AD)
-    grad_normed = (
-        grad_normed
-        + jnp.dot(grad_q16, query_back.T, preferred_element_type=jnp.float32)
-        + jnp.dot(
-            grad_kv16, keyval_back.reshape(width, 2 * AD).T, preferred_element_type=jnp.float32
-        )
-    )
-    grad_normed_sum, grad_bc_summed, grad_conv_bc_summed = (
-        lax.psum(grad_normed.astype(jnp.bfloat16), "head").astype(jnp.float32),
-        lax.psum(grad_bc_weight.astype(jnp.bfloat16), "head").astype(jnp.float32),
-        lax.psum(grad_conv_bc.astype(jnp.bfloat16), "head").astype(jnp.float32),
-    )
+    grad_in16 = jnp.concatenate([grad_zx16, grad_bc16, grad_q16, grad_kv16, grad_dt16], axis=1)
+    in_shard = scatter_sum((product_t(normed, grad_in16),))
+    shard_zx, shard_bc_part, shard_q, shard_kv, shard_dt = jnp.split(in_shard, in_ends, axis=1)
+    shard_zx = shard_zx.reshape(shard_rows, 2, inner_half)
+    shard_kv = shard_kv.reshape(shard_rows, 2, -1)
+    shard_bc = head_sum(shard_bc_part)
+    grad_normed_sum = head_sum(times_rows(grad_in16, in_full).astype(jnp.bfloat16))
     scaled_one = grad_normed_sum * norm1_gain
     grad_gain_one = jnp.sum(grad_normed_sum * x_float * norm_one, axis=0)
     x_grad = (
@@ -563,31 +555,25 @@
         + norm_one * scaled_one
         - x_float * norm_one**3 * jnp.mean(scaled_one * x_float, axis=-1, keepdims=True)
     )
-    shard_zx, shard_bc, shard_dt, shard_mout, shard_q, shard_kv, shard_ao, shard_gu, shard_down = (
-        lax.psum_scatter(grad_zx_weight, "seq", scatter_dimension=0, tiled=True),
-        lax.psum_scatter(grad_bc_summed, "seq", scatter_dimension=0, tiled=True),
-        lax.psum_scatter(grad_dt_weight, "seq", scatter_dimension=0, tiled=True),
-        lax.psum_scatter(grad_mout, "seq", scatter_dimension=1, tiled=True),
-        lax.psum_scatter(grad_q_weight, "seq", scatter_dimension=0, tiled=True),
-        lax.psum_scatter(grad_kv_weight, "seq", scatter_dimension=0, tiled=True),
-        lax.psum_scatter(grad_attn_out, "seq", scatter_dimension=1, tiled=True),
-        lax.psum_scatter(grad_gu_weight, "seq", scatter_dimension=0, tiled=True),
-        lax.psum_scatter(grad_down, "seq", scatter_dimension=1, tiled=True),
-    )
-    sum_gain_one, sum_gain_two, sum_mnorm, sum_conv_x, sum_conv_bc, sum_dt_bias, sum_skip = (
-        lax.psum(
-            (
-                grad_gain_one,
-                grad_gain_two,
-                grad_mnorm,
-                grad_conv_x,
-                grad_conv_bc_summed,
-                grad_dt_bias,
-                grad_skip,
-            ),
-            "seq",
-        )
-    )
+    small_parts = (
+        grad_gain_one,
+        grad_gain_two,
+        grad_mnorm,
+        grad_conv_x,
+        grad_conv_bc,
+        grad_dt_bias,
+        grad_skip,
+    )
+    small_sum = seq_sum(jnp.concatenate([part.reshape(-1) for part in small_parts]))
+    small_out = []
+    start = 0
+    for part in small_parts:
+        small_out.append(small_sum[start : start + part.size].reshape(part.shape))
+        start = start + part.size
+    sum_gain_one, sum_gain_two, sum_mnorm, sum_conv_x, conv_bc_part, sum_dt_bias, sum_skip = (
+        small_out
+    )
+    sum_conv_bc = head_sum(conv_bc_part)
     return (
         output,
         x_grad,

time: 1740 us -> 894 us (0.51)
  waiting for transfers between devices: 1060 us -> 559 us
  blocking collectives: 334 us -> 0 us
  starting transfers between devices: 21.6 us -> 53.9 us
  matrix products: 96.1 us -> 64.8 us
    unnamed x18 -> x9, waiting for transfers between devices: 411 us -> 0.14 us
    all_gather x6 -> x0, blocking collectives: 252 us -> none  [the longest x1 46.5 us: local(): lax.all_gather(w_bc, 'seq', axis=0, tiled=True)]
    reduce_scatter x5 -> x2, waiting for transfers between devices: 465 us -> 261 us  [scatter_sum(): lax.psum_scatter(packed, 'seq', scatter_dimension=0, tiled=True)]
    all_gather x6 -> x5, waiting for transfers between devices: 71.5 us -> 220 us  [the longest x3 143 us: local(): lax.all_gather(jnp.concatenate(parts, axis=1), 'seq', axis=0, tiled=True)]
    psum x3 -> x0, blocking collectives: 82.1 us -> none  [the longest x1 77 us: local(): lax.psum((grad_gain_one, grad_gain_two, grad_mnorm, grad_conv_x, grad_con...]
    psum x3 -> x0, waiting for transfers between devices: 59.1 us -> none  [the longest x1 41.3 us: local(): lax.psum((mamba_part, attn_part, square_part), 'head')]
    ppermute x12, starting transfers between devices: 20.5 us -> 45.9 us  [from_behind(): return lax.ppermute(block, axis, route)]
    reshape x4 -> x7, local copies, waits for them, and re-layouts: 22.7 us -> 4.45 us  [the longest x1 1.23 us: local(): shard_gu = ff_shard[:, :2 * ff_half].reshape(shard_rows, 2, ff_half)]
  transfers between devices with their start and end apart: 28 -> 32, of which waited for: 19 -> 20; matrix products, arithmetic and copies ran while one was open for 11% -> 25% of each run, Pallas kernels for 0% -> 0%
where the time goes in v1:
time: 894 us; the launch traced here: 885 us
  waiting for transfers between devices  559 us (63%)
  local copies, waits for them, and re-layouts  92.7 us (10%)
  other arithmetic  89.3 us (10%)
  matrix products  64.8 us (7%)
  starting transfers between devices  53.9 us (6%)
  between operations  17.2 us (2%)
    reduce_scatter x2, waiting for transfers between devices, scatter_sum(): lax.psum_scatter(packed, 'seq', scatter_dimension=0, tiled=True)  261 us
    all_gather x3, waiting for transfers between devices, local(): lax.all_gather(jnp.concatenate(parts, axis=1), 'seq', axis=0, tiled=True)  143 us
    all_gather x1, waiting for transfers between devices, gather_states(): gathered = lax.all_gather(packed, 'seq')  77.2 us
    ppermute x12, waiting for transfers between devices, from_behind(): return lax.ppermute(block, axis, route)  68 us
    ppermute x12, starting transfers between devices, from_behind(): return lax.ppermute(block, axis, route)  45.9 us
    unnamed x318, local copies, waits for them, and re-layouts  26 us
  transfers between devices with their start and end apart: 32, of which 20 were waited for; matrix products, arithmetic and copies ran while one was open for 25% of the time, Pallas kernels for 0%

profile of v1, /device:TPU:0, one launch (start us, length us, event | category | flops | bytes accessed | tf_op | source)
XLA Modules:
  0.0 885.0 jit_solution(14957349847107291223)
XLA Ops:
  20.6 74.2 %all-gather.9.cloned.1.call-done = bf16[1024,2188]{1,0:T(8,128)(2,1)} async-done(((bf16[64,2188]{1,0:T(8,128)(2,1)}), bf16[1024,2188]{1,0:T(8,128)(2,1)}) %all-gather.9.cloned.1.call-update) | async-done | bytes 4481040 | tf_op jit(solution)/shard_map/all_gather | solution.py:357
  94.8 4.6 fusion.136
  124.6 4.4 collective-permute-start.4
  131.0 5.7 collective-permute-start.5
  139.0 11.7 %collective-permute-start.6 = (bf16[704,128]{0,1:T(8,128)(2,1)S(1)}, bf16[704,128]{0,1:T(8,128)(2,1)S(1)}, u32[]{:S(2)}, u32[]{:S(2)}) collective-permute-start(bf16[704,128]{0,1:T(8,128)(2,1)S(1)} %maximum_maximum_fusion), channel_id=1, source_target_pairs={{0,8},{2,10},{4,12},{6,14},{8,16},{10,18},{12,20},{14,22},{16,24},... | collective-permute-start | bytes 540680 | tf_op jit(solution)/shard_map/ppermute | solution.py:28
  151.6 6.0 collective-permute-done.6
  158.0 9.0 %collective-permute-start.7 = (bf16[880,128]{0,1:T(8,128)(2,1)S(1)}, bf16[880,128]{0,1:T(8,128)(2,1)S(1)}, u32[]{:S(2)}, u32[]{:S(2)}) collective-permute-start(bf16[880,128]{0,1:T(8,128)(2,1)S(1)} %slice.603), channel_id=1, source_target_pairs={{0,16},{2,18},{4,20},{6,22},{8,24},{10,26},{12,28},{14,30},{1,17},... | collective-permute-start | bytes 675848 | tf_op jit(solution)/shard_map/ppermute | solution.py:28
  170.8 12.4 %while.64 = (s32[]{:T(128)}, f32[4,176,1]{1,0,2:T(4,128)S(1)}, f32[4,176,1]{1,0,2:T(4,128)S(1)}, pred[176,2816]{1,0:T(8,128)(4,1)}, bf16[2816,128]{0,1:T(8,128)(...) while((s32[]{:T(128)}, f32[4,176,1]{1,0,2:T(4,128)S(1)}, ...), condition=%wide.region_10.11_spmd, body=%wide.region_4.10_spmd.sunk | while | flops 67033480 | bytes 4861995 | solution.py:228
  183.3 12.1 %while.65 = (s32[]{:T(128)}, f32[176,4,64]{0,2,1:T(8,128)S(1)}, pred[176,2816]{1,0:T(8,128)(4,1)}, bf16[2816,128]{0,1:T(8,128)(2,1)S(1)}, bf16[176,4,64]{0,2,1:T...) while((s32[]{:T(128)}, f32[176,4,64]{0,2,1:T(8,128)S(1)}, ...), condition=%wide.region_15.16_spmd, body=%wide.region_11.15_spmd.sunk | while | flops 129029136 | bytes 1282835 | solution.py:245
  198.5 77.2 %all-gather.17.cloned.1.call-done = f32[16,12,8320]{2,1,0:T(8,128)} async-done(((f32[1,12,8320]{2,1,0:T(8,128)}), f32[16,12,8320]{2,1,0:T(8,128)}) %all-gather.17.cloned.1.call-update) | async-done | bytes 6389776 | tf_op jit(solution)/shard_map/all_gather | solution.py:36
  277.4 4.3 fusion.33
  301.6 68.8 %all-gather.13.cloned.1.call-done = bf16[1024,3072]{1,0:T(8,128)(2,1)} async-done(((bf16[64,3072]{1,0:T(8,128)(2,1)}), bf16[1024,3072]{1,0:T(8,128)(2,1)}) %all-gather.13.cloned.1.call-update) | async-done | bytes 6291472 | tf_op jit(solution)/shard_map/all_gather | solution.py:357
  410.1 38.8 %while.66 = (s32[]{:T(128)}, f32[176,4,64]{0,2,1:T(8,128)}, f32[2816,128]{0,1:T(8,128)}, pred[176,2816]{1,0:T(8,128)(4,1)}, bf16[2816,128]{0,1:T(8,128)(2,1)}, /...) while((s32[]{:T(128)}, f32[176,4,64]{0,2,1:T(8,128)}, ...), condition=%wide.region_27.28_spmd.clone, body=%wide.region_22.27_spmd.clone.sunk | while | flops 322724160 | bytes 14057327 | solution.py:529
  437.1 7.0 conditional.9
  459.9 25.1 %collective-permute-done.13 = bf16[880,128]{0,1:T(8,128)(2,1)S(1)} collective-permute-done((bf16[880,128]{0,1:T(8,128)(2,1)S(1)}, bf16[880,128]{0,1:T(8,128)(2,1)S(1)}, u32[]{:S(2)}, u32[]{:S(2)}) %collective-permute-start.13) | collective-permute-done | bytes 225312 | tf_op jit(solution)/shard_map/ppermute | solution.py:28
  490.7 7.4 collective-permute-done.14
  500.4 8.3 collective-permute-done.15
  511.0 4.5 collective-permute-done.16
  521.6 5.4 multiply_reduce_fusion.11
  541.6 4.4 scatter-add.31
  546.4 4.4 scatter-add.34
  556.6 11.7 %collective-permute-done.11 = f32[3,768]{0,1:T(8,128)} collective-permute-done((f32[3,768]{0,1:T(8,128)}, f32[3,768]{0,1:T(8,128)}, u32[]{:S(2)}, u32[]{:S(2)}) %collective-permute-start.11) | collective-permute-done | bytes 9248 | tf_op jit(solution)/shard_map/ppermute | solution.py:28
  591.9 132.8 %reduce-scatter.8.cloned.1.call-done = bf16[64,3072]{1,0:T(8,128)(2,1)} async-done(((bf16[1024,3072]{1,0:T(8,128)(2,1)}), bf16[64,3072]{1,0:T(8,128)(2,1)}) %reduce-scatter.8.cloned.1.call-update) | async-done | bytes 393232 | tf_op jit(solution)/shard_map/reduce_scatter | solution.py:289
  739.7 128.6 %reduce-scatter.6.cloned.1.call-done = bf16[64,2188]{1,0:T(8,128)(2,1)} async-done(((bf16[1024,2188]{1,0:T(8,128)(2,1)}), bf16[64,2188]{1,0:T(8,128)(2,1)}) %reduce-scatter.6.cloned.1.call-update) | async-done | bytes 280080 | tf_op jit(solution)/shard_map/reduce_scatter | solution.py:289
  (633 shorter events, 265.9 us)
Async XLA Ops:
  7.2 87.6 %all-gather.9.cloned.1.call-start = ((), (), s32[]{:S(2)}) async-start(), calls=%async_computation.3 | async-start | bytes 5013504 | tf_op jit(solution)/shard_map/all_gather | solution.py:357
  12.3 183.9 %all-gather.11.cloned.1.call-start = ((), (), s32[]{:S(2)}) async-start(), calls=%async_computation.4 | async-start | bytes 2228224 | tf_op jit(solution)/shard_map/all_gather | solution.py:357
  13.9 261.7 %all-gather.17.cloned.1.call-start = ((), (), s32[]{:S(2)}) async-start(), calls=%async_computation.9 | async-start | bytes 9052160 | tf_op jit(solution)/shard_map/all_gather | solution.py:36
  102.0 8.6 collective-permute-start.1
  105.3 6.6 collective-permute-start
  117.2 253.3 %all-gather.13.cloned.1.call-start = ((), (), s32[]{:S(2)}) async-start(), calls=%async_computation.5 | async-start | bytes 6684672 | tf_op jit(solution)/shard_map/all_gather | solution.py:357
  119.9 396.0 %all-gather.15.cloned.1.call-start = ((), (), s32[]{:S(2)}) async-start(), calls=%async_computation.8 | async-start | bytes 6684672 | tf_op jit(solution)/shard_map/all_gather | solution.py:478
  124.6 6.3 collective-permute-start.4
  131.0 7.9 collective-permute-start.5
  139.0 18.6 %collective-permute-start.6 = (bf16[704,128]{0,1:T(8,128)(2,1)S(1)}, bf16[704,128]{0,1:T(8,128)(2,1)S(1)}, u32[]{:S(2)}, u32[]{:S(2)}) collective-permute-start(bf16[704,128]{0,1:T(8,128)(2,1)S(1)} %maximum_maximum_fusion), channel_id=1, source_target_pairs={{0,8},{2,10},{4,12},{6,14},{8,16},{10,18},{12,20},{14,22},{16,24},... | collective-permute-start | bytes 540680 | tf_op jit(solution)/shard_map/ppermute | solution.py:28
  158.0 12.3 %collective-permute-start.7 = (bf16[880,128]{0,1:T(8,128)(2,1)S(1)}, bf16[880,128]{0,1:T(8,128)(2,1)S(1)}, u32[]{:S(2)}, u32[]{:S(2)}) collective-permute-start(bf16[880,128]{0,1:T(8,128)(2,1)S(1)} %slice.603), channel_id=1, source_target_pairs={{0,16},{2,18},{4,20},{6,22},{8,24},{10,26},{12,28},{14,30},{1,17},... | collective-permute-start | bytes 675848 | tf_op jit(solution)/shard_map/ppermute | solution.py:28
  198.5 99.5 %collective-permute-start.8 = (f32[176,1024]{1,0:T(8,128)}, f32[176,1024]{1,0:T(8,128)}, u32[]{:S(2)}, u32[]{:S(2)}) collective-permute-start(f32[176,1024]{1,0:T(8,128)} %fusion.107), channel_id=1, source_target_pairs={{0,1},{1,0},{2,3},{3,2},{4,5},{5,4},{6,7},{7,6},{8,9},{9,8},{10,11... | collective-permute-start | bytes 2162696 | tf_op jit(solution)/shard_map/ppermute | solution.py:59
  388.9 191.7 %reduce-scatter.10.cloned.1.call-start = ((), (), s32[]{:S(2)}) async-start(), calls=%async_computation.10 | async-start | bytes 2228224
  397.2 327.6 %reduce-scatter.8.cloned.1.call-start = ((), (), s32[]{:S(2)}) async-start(), calls=%async_computation.7 | async-start | bytes 6684672 | tf_op jit(solution)/shard_map/reduce_scatter | solution.py:289
  403.7 464.6 %reduce-scatter.6.cloned.1.call-start = ((), (), s32[]{:S(2)}) async-start(), calls=%async_computation.6 | async-start | bytes 5013504 | tf_op jit(solution)/shard_map/reduce_scatter | solution.py:289
  451.3 33.6 %collective-permute-start.13 = (bf16[880,128]{0,1:T(8,128)(2,1)S(1)}, bf16[880,128]{0,1:T(8,128)(2,1)S(1)}, u32[]{:S(2)}, u32[]{:S(2)}) collective-permute-start(bf16[880,128]{0,1:T(8,128)(2,1)S(1)} %slice.752), channel_id=1, source_target_pairs={{16,0},{18,2},{20,4},{22,6},{24,8},{26,10},{28,12},{30,14},{17,1},... | collective-permute-start | bytes 675848 | tf_op jit(solution)/shard_map/ppermute | solution.py:28
  489.2 8.9 %collective-permute-start.14 = (bf16[704,128]{0,1:T(8,128)(2,1)S(1)}, bf16[704,128]{0,1:T(8,128)(2,1)S(1)}, u32[]{:S(2)}, u32[]{:S(2)}) collective-permute-start(bf16[704,128]{0,1:T(8,128)(2,1)S(1)} %slice.753), channel_id=1, source_target_pairs={{8,0},{10,2},{12,4},{14,6},{16,8},{18,10},{20,12},{22,14},{24,16},... | collective-permute-start | bytes 540680 | tf_op jit(solution)/shard_map/ppermute | solution.py:28
  498.3 10.4 %collective-permute-start.15 = (bf16[352,128]{0,1:T(8,128)(2,1)S(1)}, bf16[352,128]{0,1:T(8,128)(2,1)S(1)}, u32[]{:S(2)}, u32[]{:S(2)}) collective-permute-start(bf16[352,128]{0,1:T(8,128)(2,1)S(1)} %slice.754), channel_id=1, source_target_pairs={{4,0},{6,2},{8,4},{10,6},{12,8},{14,10},{16,12},{18,14},{20,16},{2... | collective-permute-start | bytes 270344 | tf_op jit(solution)/shard_map/ppermute | solution.py:28
  508.9 6.7 collective-permute-start.16
  536.2 19.3 %collective-permute-start.12 = (f32[3,256]{0,1:T(8,128)}, f32[3,256]{0,1:T(8,128)S(1)}, u32[]{:S(2)}, u32[]{:S(2)}) collective-permute-start(f32[3,256]{0,1:T(8,128)} %slice.615), channel_id=1, source_target_pairs={{2,0},{4,2},{6,4},{8,6},{10,8},{12,10},{14,12},{16,14},{18,16},{20... | collective-permute-start | bytes 9224 | tf_op jit(solution)/shard_map/ppermute | solution.py:28
  551.5 16.8 %collective-permute-start.11 = (f32[3,768]{0,1:T(8,128)}, f32[3,768]{0,1:T(8,128)}, u32[]{:S(2)}, u32[]{:S(2)}) collective-permute-start(f32[3,768]{0,1:T(8,128)} %slice.611), channel_id=1, source_target_pairs={{2,0},{4,2},{6,4},{8,6},{10,8},{12,10},{14,12},{16,14},{18,16},{20... | collective-permute-start | bytes 27656 | tf_op jit(solution)/shard_map/ppermute | solution.py:28
  588.1 137.7 %collective-permute-start.19 = (f32[6936]{0:T(1024)S(1)}, f32[6936]{0:T(1024)S(1)}, u32[]{:S(2)}, u32[]{:S(2)}) collective-permute-start(f32[6936]{0:T(1024)S(1)} %concatenate.135), channel_id=1, source_target_pairs={{0,2},{2,0},{4,6},{6,4},{8,10},{10,8},{12,14},{14,12},{16,18},{18,... | collective-permute-start | bytes 83240 | tf_op jit(solution)/shard_map/ppermute | solution.py:68
  739.7 131.9 %collective-permute-start.23 = (f32[4,256]{1,0:T(4,128)S(1)}, f32[4,256]{1,0:T(4,128)S(1)}, u32[]{:S(2)}, u32[]{:S(2)}) collective-permute-start(f32[4,256]{1,0:T(4,128)S(1)} %reshape.869), channel_id=1, source_target_pairs={{0,1},{1,0},{2,3},{3,2},{4,5},{5,4},{6,7},{7,6},{8,9},{9,8},{10,11... | collective-permute-start | bytes 12296 | tf_op jit(solution)/shard_map/ppermute | solution.py:59
  869.8 7.3 collective-permute-start.18
  (160 other events, 3414.4 us)
Sparse Core Ops, SparseCore 0:
  12.4 82.3 all-gather.8
  98.2 60.5 all-gather.10
  161.5 114.1 all-gather.16
  278.9 91.5 all-gather.12
  389.0 99.6 all-gather.14
  490.9 83.1 reduce-scatter.9
  579.3 145.3 reduce-scatter.7
  729.9 138.3 reduce-scatter.5
